TPU v7x, 128 devices: a whole 4x4x4 slice. The times are simulated.
128 devices in a mesh: replica: 4 (over y_hi, core), fsdp: 32 (over y_lo, z, x).
Axes of the slice: x: 4, y: 4 (y_hi: 2, y_lo: 2; y = y_hi * 2 + y_lo), z: 4, core: 2. Of those that a mesh axis runs over, the one named last changes fastest.
Arguments:
- layer_input: bfloat16 [4, 16384, 4096], P('replica', 'fsdp'), may hold values from -36 to 36, as said below
- norm_gain: bfloat16 [4, 4096], P('replica', 'fsdp'), may hold values from 0.099609375 to 1.8984375
- kv_weight: bfloat16 [4, 4096, 1024], P('replica', 'fsdp'), may hold values from -0.09375 to 0.09375
- kv_cotangent: bfloat16 [4, 16384, 1024], P('replica', 'fsdp'), may hold values from -6 to 6
- pseudo_grad: float32 [4, 12288, 1024], P('replica', 'fsdp'), may hold values from -6 to 6
- outer_momentum: float32 [12288, 1024], P('fsdp'), may hold values from -6 to 6
- global_params: float32 [12288, 1024], P('fsdp'), may hold values from -6 to 6
- local_params: bfloat16 [4, 12288, 1024], P('replica', 'fsdp'), may hold values from -6 to 6
Outputs:
- kv_out: bfloat16 [4, 16384, 1024], P('replica', 'fsdp')
- input_grad: bfloat16 [4, 16384, 4096], P('replica', 'fsdp')
- kv_weight_grad: float32 [4, 4096, 1024], P('replica', 'fsdp')
- gain_grad: float32 [4, 4096], P('replica', 'fsdp')
- momentum_new: float32 [12288, 1024], P('fsdp')
- global_new: float32 [12288, 1024], P('fsdp')
- local_new: bfloat16 [4, 12288, 1024], P('replica', 'fsdp')
Inputs may be any that keep to these rules, and one draw needn't show every extreme that they name: `layer_input`: activations of the residual stream.
All inputs are finite; a program needn't handle non-finite values.
Results may differ from a plain program's by a relative error of at most 0.0049.
Values may be sent and summed in bfloat16 or wider, within the bound.
A program may use at most 128 MiB of HBM per device.

v0:
```python
import math
import jax
import jax.numpy as jnp
from jax import lax
from jax.sharding import PartitionSpec as P

HEAD = 128
SEQ_LEN = 4096
epsilon = 1e-05
rope_base = 500000.0
momentum_rate = 0.9
outer_rate = 0.7
mixing_rate = 0.5


def angles_for(positions, head):
    half = head // 2
    index_f = jnp.arange(half, dtype=jnp.float32)
    inverse = jnp.exp(index_f * (-2.0 * math.log(rope_base) / head))
    angle = positions.astype(jnp.float32)[:, None] * inverse[None, :]
    return (jnp.cos(angle), jnp.sin(angle))


def rotate_keys(keys, cosine, sine, head, sign):
    count = keys.shape[0]
    shaped = keys.reshape(count, -1, head)
    half = head // 2
    first = shaped[:, :, :half]
    second = shaped[:, :, half:]
    cos_b = cosine[:, None, :]
    sin_b = sine[:, None, :] * sign
    out = jnp.concatenate([first * cos_b - second * sin_b, second * cos_b + first * sin_b], axis=2)
    return out.reshape(count, -1)


def forward_piece(normed, weight_piece, gain_piece):
    gain_vals = gain_piece.astype(jnp.float32)
    hidden_piece = (normed * gain_vals[None, :]).astype(jnp.bfloat16)
    key_pre = jnp.dot(hidden_piece, weight_piece, preferred_element_type=jnp.float32)
    return (key_pre, hidden_piece, gain_vals)


def backward_piece(kv_grad, weight_piece):
    product = lax.dot_general(
        kv_grad, weight_piece, (((1,), (1,)), ((), ())), preferred_element_type=jnp.float32
    )
    return product


def local(
    layer_input,
    norm_gain,
    kv_weight,
    kv_cotangent,
    pseudo_grad,
    outer_momentum,
    global_params,
    local_params,
):
    tokens_in = layer_input[0]
    gain_shard = norm_gain[0]
    weight_shard = kv_weight[0]
    cotangent = kv_cotangent[0]
    rows, width = tokens_in.shape
    kvw = weight_shard.shape[1] // 2
    groups = lax.axis_size("fsdp")
    positions = (lax.axis_index("fsdp") * rows + jnp.arange(rows, dtype=jnp.int32)) % SEQ_LEN
    cosine, sine = angles_for(positions, HEAD)
    values = tokens_in.astype(jnp.float32)
    inv_rms = lax.rsqrt(jnp.mean(values * values, axis=-1, keepdims=True) + epsilon)
    normed = values * inv_rms
    key_back = rotate_keys(cotangent[:, :kvw].astype(jnp.float32), cosine, sine, HEAD, -1.0).astype(
        jnp.bfloat16
    )
    kv_grad = jnp.concatenate([key_back, cotangent[:, kvw:]], axis=1)
    key_pre, hidden, gain_full = forward_piece(
        normed,
        lax.all_gather(weight_shard, "fsdp", axis=0, tiled=True),
        lax.all_gather(gain_shard, "fsdp", axis=0, tiled=True),
    )
    hidden_grad = backward_piece(kv_grad, lax.all_gather(weight_shard, "fsdp", axis=0, tiled=True))
    kv_out = jnp.concatenate(
        [rotate_keys(key_pre[:, :kvw], cosine, sine, HEAD, 1.0), key_pre[:, kvw:]], axis=1
    ).astype(jnp.bfloat16)
    scale = 1.0 / math.sqrt(rows * groups)
    gain_product = hidden_grad * normed
    weight_term = (
        lax.dot_general(
            hidden, kv_grad, (((0,), (0,)), ((), ())), preferred_element_type=jnp.float32
        )
        * scale
    )
    gain_term = jnp.sum(gain_product, axis=0) * scale
    weight_grad, gain_grad = (
        lax.psum_scatter(weight_term, "fsdp", scatter_dimension=0, tiled=True),
        lax.psum_scatter(gain_term, "fsdp", scatter_dimension=0, tiled=True),
    )
    normed_grad = hidden_grad * gain_full
    input_grad = (
        inv_rms * (normed_grad - normed * jnp.mean(normed_grad * normed, axis=-1, keepdims=True))
    ).astype(jnp.bfloat16)
    pseudo = pseudo_grad[0]
    replicas = lax.axis_size("replica")
    total = lax.psum(pseudo, "replica")
    average = total / replicas
    momentum_new = momentum_rate * outer_momentum + average
    global_new = global_params - outer_rate * (average + momentum_rate * momentum_new)
    local_new = (
        mixing_rate * local_params[0].astype(jnp.float32) + (1.0 - mixing_rate) * global_new
    ).astype(jnp.bfloat16)
    return (
        kv_out[None],
        input_grad[None],
        weight_grad[None],
        gain_grad[None],
        momentum_new,
        global_new,
        local_new[None],
    )


def solution(mesh):
    in_specs = (
        P("replica", "fsdp", None),
        P("replica", "fsdp"),
        P("replica", "fsdp", None),
        P("replica", "fsdp", None),
        P("replica", "fsdp", None),
        P("fsdp", None),
        P("fsdp", None),
        P("replica", "fsdp", None),
    )
    out_specs = (
        P("replica", "fsdp", None),
        P("replica", "fsdp", None),
        P("replica", "fsdp", None),
        P("replica", "fsdp"),
        P("fsdp", None),
        P("fsdp", None),
        P("replica", "fsdp", None),
    )
    return jax.shard_map(local, mesh=mesh, in_specs=in_specs, out_specs=out_specs, check_vma=False)
```

profile of v0, /device:TPU:0, one launch (start us, length us, event | category | flops | bytes accessed | tf_op | source)
XLA Modules:
  0.0 415.8 jit_solution(27503207839580185)
XLA Ops:
  8.0 0.0 copy-start.3
  8.0 0.0 all-gather.4.cloned.1.call-start
  8.1 0.7 all-gather.4.cloned.1.call-update
  8.7 0.0 all-reduce.3.cloned.1.call-start
  8.8 0.5 all-reduce.3.cloned.1.call-update
  9.3 0.0 reduce-scatter.2.cloned.1.call-start
  9.4 82.9 %all-gather = bf16[1,4096]{1,0:T(2,128)(2,1)S(1)} all-gather(bf16[1,128]{1,0:T(2,128)(2,1)} %param.9), channel_id=2, replica_groups=mesh['replica'=4,'fsdp'=32] {'fsdp'}, dimensions={1}, use_global_device_ids=true | all-gather | bytes 8448 | tf_op jit(solution)/shard_map/all_gather | solution.py:79
  92.3 3.1 fusion.10
  95.4 0.0 copy-done.3
  95.5 0.9 slice_convert_fusion.1
  96.4 0.4 reshape.172
  96.8 1.8 broadcast_multiply_fusion.1
  98.6 80.9 %all-gather.4.cloned.1.call-done = bf16[1,4096,1024]{2,1,0:T(8,128)(2,1)} async-done(((bf16[1,128,1024]{2,1,0:T(8,128)(2,1)}), bf16[1,4096,1024]{2,1,0:T(8,128)(2,1)}) %all-gather.4.cloned.1.call-update) | async-done | bytes 8388624 | tf_op jit(solution)/shard_map/all_gather | solution.py:78
  179.5 8.2 %fusion.13 = f32[512,1024]{1,0:T(8,128)S(1)} fusion(bf16[1,4096,1024]{2,1,0:T(8,128)(2,1)} %all-gather.4.cloned.1.call-done, bf16[1,512,4096]{2,1,0:T(8,128)(2,1)} %param.8, f32[4096]{0:T(1024)S(1)} %bitcast.41, f32[512]{0:T(512)S(1)} %add_rsqrt_fusion), kind=kOutput, calls=%fused_computation.15 | convolution fusion | flops 4303355904 | bytes 14698496 | tf_op jit(solution)/shard_map/dot_general | solution.py:39
  187.7 0.0 copy-start.2
  187.7 1.3 copy-done.2
  189.1 0.1 slice.33
  189.1 0.4 reshape.167
  189.5 0.0 copy-start
  189.5 0.0 copy-start.5
  189.5 2.7 subtract_convert_fusion
  192.3 1.4 pad_maximum_fusion.4
  193.7 0.1 copy.17
  193.8 0.0 copy-start.7
  193.8 0.0 copy-done
  193.8 0.0 copy-done.5
  193.8 8.3 %broadcast_multiply_fusion = f32[4096,1024]{1,0:T(8,128)} fusion(bf16[1,512,4096]{2,1,0:T(8,128)(2,1)S(1)} %copy-done, f32[4096]{0:T(1024)S(1)} %bitcast.42, f32[512]{0:T(512)S(1)} %add_rsqrt_fusion, bf16[512,512]{1,0:T(8,128)(2,1)S(1)} %copy-done.5, bf16[512,512]{1,0:T(8,128)(2,1)S(1)} %bitcast.39), kind=kOutput, calls=%fused_computation.17 | convolution fusion | flops 4309647360 | bytes 22038528 | tf_op jit(solution)/shard_map/dot_general | solution.py:88
  202.1 0.0 copy-done.7
  202.1 0.0 copy-start.8
  202.1 0.0 copy-start.1
  202.1 0.0 copy-start.4
  202.1 0.0 reduce-scatter.2.cloned.1.call-update
  202.1 0.6 copy-done.8
  202.8 0.6 dynamic-slice
  204.0 0.0 copy-start.6
  204.0 0.0 all-reduce.3.cloned.1.call-done
  204.0 0.0 copy-done.1
  204.1 0.0 copy-done.4
  204.1 4.6 %fusion.20 = (bf16[1,384,1024]{2,1,0:T(8,128)(2,1)}, f32[384,1024]{1,0:T(8,128)}, f32[384,1024]{1,0:T(8,128)}) fusion(bf16[1,384,1024]{2,1,0:T(8,128)(2,1)S(1)} %copy-done.4, f32[384,1024]{1,0:T(8,128)S(1)} %copy-done.1, f32[384,1024]{1,0:T(8,128)} %all-reduce.3.cloned.1.call-done, f32[384,1024]{1,0:T(8,128)} %param.13), kind=kLoop, calls=%fused_computation.31 | loop fusion | flops 4325376 | bytes 9437184 | tf_op jit(solution)/shard_map/broadcast_in_dim | solution.py:118
  208.7 0.2 concatenate.27
  208.9 0.0 copy-done.6
  208.9 13.6 %fusion.9 = (f32[4096]{0:T(1024)S(1)}, f32[512]{0:T(512)S(1)}, f32[512,4096]{1,0:T(8,128)}) fusion(bf16[1,512,4096]{2,1,0:T(8,128)(2,1)} %param.8, f32[512]{0:T(512)S(1)} %add_rsqrt_fusion, f32[4096]{0:T(1024)S(1)} %bitcast.43, bf16[1,4096,1024]{2,1,0:T(8,128)(2,1)} %all-gather.4.cloned.1.call-done, bf16[512,512]{1,0:T(8,128)(2,1)S(1)} %copy-done.6, ...), kind=kOutput, calls=%fused_computation.11 | convolution fusion | flops 4311739904 | bytes 22056960 | tf_op jit(solution)/shard_map/dot_general | solution.py:44
  222.4 158.3 %all-reduce = f32[4096]{0:T(1024)S(1)} all-reduce(f32[4096]{0:T(1024)S(1)} %broadcast_multiply_fusion.2), channel_id=5, replica_groups=mesh['replica'=4,'fsdp'=32] {'fsdp'}, use_global_device_ids=true, to_apply=%region_4.5.clone | all-reduce | flops 4096 | bytes 32768
  380.8 0.6 dynamic-slice_bitcast_fusion
  381.3 1.3 fusion.21
  382.6 1.1 pad_maximum_fusion
  383.8 7.3 %fusion.15 = bf16[1,512,4096]{2,1,0:T(8,128)(2,1)} fusion(f32[512,4096]{1,0:T(8,128)} %get-tuple-element.23, bf16[1,512,4096]{2,1,0:T(8,128)(2,1)} %param.8, f32[512]{0:T(512)S(1)} %broadcast_multiply_fusion.3, f32[4096]{0:T(1024)S(1)} %bitcast.44, f32[512]{0:T(512)S(1)} %add_rsqrt_fusion), kind=kLoop, calls=%fused_computation.18 | loop fusion | flops 14680064 | bytes 16797696 | tf_op jit(solution)/shard_map/broadcast_in_dim | solution.py:113
  391.1 17.3 %reduce-scatter.2.cloned.1.call-done = f32[128,1024]{1,0:T(8,128)} async-done(((f32[4096,1024]{1,0:T(8,128)}), f32[128,1024]{1,0:T(8,128)}) %reduce-scatter.2.cloned.1.call-update) | async-done | bytes 524304 | tf_op jit(solution)/shard_map/reduce_scatter | solution.py:95
  (6 shorter events, 0.1 us)
Async XLA Ops:
  8.0 87.4 %copy-start.3 = (bf16[1,512,1024]{2,1,0:T(8,128)(2,1)S(1)}, bf16[1,512,1024]{2,1,0:T(8,128)(2,1)}, u32[]{:S(2)}) copy-start(bf16[1,512,1024]{2,1,0:T(8,128)(2,1)} %param.11) | copy-start | bytes 3145732
  8.0 171.5 %all-gather.4.cloned.1.call-start = ((), (), s32[]{:S(2)}) async-start(), calls=%async_computation.3 | async-start | bytes 8650752 | tf_op jit(solution)/shard_map/all_gather | solution.py:78
  8.7 195.3 %all-reduce.3.cloned.1.call-start = ((), (), s32[]{:S(2)}) async-start(), calls=%async_computation.2 | async-start | bytes 3145728 | tf_op jit(solution)/shard_map/psum | solution.py:104
  9.3 399.1 %reduce-scatter.2.cloned.1.call-start = ((), (), s32[]{:S(2)}) async-start(), calls=%async_computation.1 | async-start | bytes 17301504 | tf_op jit(solution)/shard_map/reduce_scatter | solution.py:95
  187.7 1.3 copy-start.2
  189.5 4.3 %copy-start = (bf16[1,512,4096]{2,1,0:T(8,128)(2,1)S(1)}, bf16[1,512,4096]{2,1,0:T(8,128)(2,1)}, u32[]{:S(2)}) copy-start(bf16[1,512,4096]{2,1,0:T(8,128)(2,1)} %param.8) | copy-start | bytes 12582916
  189.5 4.3 %copy-start.5 = (bf16[512,512]{1,0:T(8,128)(2,1)S(1)}, bf16[512,512]{1,0:T(8,128)(2,1)}, u32[]{:S(2)}) copy-start(bf16[512,512]{1,0:T(8,128)(2,1)} %get-tuple-element.17) | copy-start | bytes 1572868
  193.8 8.3 %copy-start.7 = (bf16[64,8,4,128]{3,1,2,0:T(8,128)(2,1)}, bf16[64,8,4,128]{3,1,2,0:T(8,128)(2,1)S(1)}, u32[]{:S(2)}) copy-start(bf16[64,8,4,128]{3,1,2,0:T(8,128)(2,1)S(1)} %copy.17) | copy-start | bytes 1572868
  202.1 0.7 copy-start.8
  202.1 1.9 copy-start.1
  202.1 1.9 copy-start.4
  204.0 4.9 %copy-start.6 = (bf16[512,512]{1,0:T(8,128)(2,1)S(1)}, bf16[512,512]{1,0:T(8,128)(2,1)}, u32[]{:S(2)}) copy-start(bf16[512,512]{1,0:T(8,128)(2,1)} %get-tuple-element.17) | copy-start | bytes 1572868
Sparse Core Ops, SparseCore 0:
  10.5 168.9 all-gather.3
  202.3 206.0 reduce-scatter.1
Sparse Core Ops, SparseCore 1:
  11.7 70.8 all-reduce.2
where the time goes:
time: 416 us
  blocking collectives  241 us (58%)
  waiting for transfers between devices  99.4 us (24%)
  matrix products  30.1 us (7%)
  other arithmetic  23.1 us (6%)
  between operations  16.3 us (4%)
  local copies, waits for them, and re-layouts  5.51 us (1%)
    unnamed x1, blocking collectives  158 us
    all_gather x1, blocking collectives, local(): lax.all_gather(gain_shard, 'fsdp', axis=0, tiled=True)  82.9 us
    all_gather x1, waiting for transfers between devices, local(): lax.all_gather(weight_shard, 'fsdp', axis=0, tiled=True)  80.9 us
    reduce_scatter x1, waiting for transfers between devices, local(): lax.psum_scatter(weight_term, 'fsdp', scatter_dimension=0, tiled=True)  17.3 us
    dot_general x1, matrix products, backward_piece(): lax.dot_general(kv_grad, weight_piece, (((1,), (1,)), ((), ())), preferre...  13.6 us
  transfers between devices with their start and end apart: 3, of which 2 were waited for; matrix products, arithmetic and copies ran while one was open for 14% of the time, Pallas kernels for 0%

commit v1 on v0

--- a/solution.py
+++ b/solution.py
@@ -75,7 +75,9 @@
     kv_grad = jnp.concatenate([key_back, cotangent[:, kvw:]], axis=1)
     key_pre, hidden, gain_full = forward_piece(
         normed,
-        lax.all_gather(weight_shard, "fsdp", axis=0, tiled=True),
+        jnp.concatenate(
+            lax.all_to_all(jnp.stack([weight_shard] * lax.axis_size("fsdp")), "fsdp", 0, 0), axis=0
+        ),
         lax.all_gather(gain_shard, "fsdp", axis=0, tiled=True),
     )
     hidden_grad = backward_piece(kv_grad, lax.all_gather(weight_shard, "fsdp", axis=0, tiled=True))

time: 416 us -> 496 us (1.19)
  blocking collectives: 241 us -> 384 us
  waiting for transfers between devices: 99.4 us -> 22.7 us
  starting transfers between devices: 0.12 us -> 9.67 us
  local copies, waits for them, and re-layouts: 5.51 us -> 10.8 us
    all_gather x1, blocking collectives: 82.9 us -> 231 us  [local(): lax.all_gather(gain_shard, 'fsdp', axis=0, tiled=True)]
    all_gather x1, waiting for transfers between devices: 80.9 us -> 0.01 us  [local(): lax.all_gather(weight_shard, 'fsdp', axis=0, tiled=True)]
    all_to_all x0 -> x1, starting transfers between devices: none -> 9.55 us  [local(): lax.all_to_all(jnp.stack([weight_shard] * lax.axis_size('fsdp')), 'fsdp',...]
    another operation x0 -> x1, local copies, waits for them, and re-layouts: none -> 5.26 us  [local(): jnp.stack([weight_shard] * lax.axis_size('fsdp'))]
    unnamed x1, blocking collectives: 158 us -> 153 us
  transfers between devices with their start and end apart: 3 -> 4, of which waited for: 2 -> 1; matrix products, arithmetic and copies ran while one was open for 14% -> 12% of each run, Pallas kernels for 0% -> 0%
where the time goes in v1:
time: 496 us; the launch traced here: 495 us
  blocking collectives  384 us (77%)
  matrix products  28.3 us (6%)
  other arithmetic  23.1 us (5%)
  waiting for transfers between devices  22.7 us (5%)
  between operations  16.3 us (3%)
  local copies, waits for them, and re-layouts  10.8 us (2%)
  starting transfers between devices  9.67 us (2%)
    all_gather x1, blocking collectives, local(): lax.all_gather(gain_shard, 'fsdp', axis=0, tiled=True)  231 us
    unnamed x1, blocking collectives  153 us
    reduce_scatter x1, waiting for transfers between devices, local(): lax.psum_scatter(weight_term, 'fsdp', scatter_dimension=0, tiled=True)  21.4 us
    dot_general x1, matrix products, backward_piece(): lax.dot_general(kv_grad, weight_piece, (((1,), (1,)), ((), ())), preferre...  11.8 us
  transfers between devices with their start and end apart: 4, of which 1 were waited for; matrix products, arithmetic and copies ran while one was open for 12% of the time, Pallas kernels for 0%

profile of v1, /device:TPU:0, one launch (start us, length us, event | category | flops | bytes accessed | tf_op | source)
XLA Modules:
  0.0 495.3 jit_solution(16366300717158978435)
XLA Ops:
  8.0 0.0 all-reduce.3.cloned.1.call-start
  8.0 0.7 all-reduce.3.cloned.1.call-update
  8.7 0.0 all-gather.4.cloned.1.call-start
  8.8 0.5 all-gather.4.cloned.1.call-update
  9.3 5.3 %stack.3 = bf16[32,128,1024]{2,1,0:T(8,128)(2,1)} broadcast(bf16[128,1024]{1,0:T(8,128)(2,1)} %bitcast.64), dimensions={1,2} | broadcast | bytes 8650752 | tf_op jit(solution)/shard_map/stack | solution.py:79
  14.6 0.0 copy-start.7
  14.6 0.0 copy-start.3
  14.6 9.5 %all-to-all-start = ((bf16[32,128,1024]{2,1,0:T(8,128)(2,1)}), bf16[32,128,1024]{2,1,0:T(8,128)(2,1)}, u32[]{:S(2)}, u32[]{:S(2)}) async-start(bf16[32,128,1024]{2,1,0:T(8,128)(2,1)} %stack.3), calls=%async_computation | async-start | bytes 16777216 | tf_op jit(solution)/shard_map/all_to_all | solution.py:79
  24.1 0.0 reduce-scatter.2.cloned.1.call-start
  24.2 0.0 copy-done.7
  24.2 231.1 %all-gather = bf16[1,4096]{1,0:T(2,128)(2,1)S(1)} all-gather(bf16[1,128]{1,0:T(2,128)(2,1)S(1)} %copy-done.7), channel_id=2, replica_groups=mesh['replica'=4,'fsdp'=32] {'fsdp'}, dimensions={1}, use_global_device_ids=true | all-gather | bytes 8448 | tf_op jit(solution)/shard_map/all_gather | solution.py:81
  255.3 0.0 copy-done.3
  255.4 0.9 slice_convert_fusion.1
  256.3 0.4 reshape.191
  256.7 3.1 fusion.12
  259.8 2.0 broadcast_multiply_fusion.1
  261.8 0.0 all-to-all-done
  261.8 8.2 %fusion.18 = f32[512,1024]{1,0:T(8,128)S(1)} fusion(bf16[4096,1024]{1,0:T(8,128)(2,1)} %bitcast.4, bf16[1,512,4096]{2,1,0:T(8,128)(2,1)} %param.8, f32[4096]{0:T(1024)S(1)} %bitcast.68, f32[512]{0:T(512)S(1)} %add_rsqrt_fusion), kind=kOutput, calls=%fused_computation.21 | convolution fusion | flops 4303355904 | bytes 14698496 | tf_op jit(solution)/shard_map/dot_general | solution.py:39
  270.0 0.0 copy-start.2
  270.0 1.3 copy-done.2
  271.3 0.1 slice.33
  271.4 0.4 reshape.186
  271.8 0.0 copy-start
  271.8 0.0 copy-start.5
  271.8 2.7 subtract_convert_fusion
  274.6 1.4 pad_maximum_fusion.4
  276.0 0.1 copy.17
  276.1 0.0 copy-done
  276.1 0.0 copy-done.5
  276.1 8.3 %broadcast_multiply_fusion = f32[4096,1024]{1,0:T(8,128)} fusion(bf16[1,512,4096]{2,1,0:T(8,128)(2,1)S(1)} %copy-done, f32[4096]{0:T(1024)S(1)} %bitcast.69, f32[512]{0:T(512)S(1)} %add_rsqrt_fusion, bf16[512,512]{1,0:T(8,128)(2,1)S(1)} %copy-done.5, bf16[512,512]{1,0:T(8,128)(2,1)S(1)} %bitcast.66), kind=kOutput, calls=%fused_computation.19 | convolution fusion | flops 4309647360 | bytes 22038528 | tf_op jit(solution)/shard_map/dot_general | solution.py:90
  284.4 0.0 copy-start.8
  284.4 0.0 copy-start.1
  284.4 0.0 copy-start.4
  284.4 0.0 reduce-scatter.2.cloned.1.call-update
  284.4 0.6 copy-done.8
  285.1 0.6 dynamic-slice
  286.3 0.0 all-reduce.3.cloned.1.call-done
  286.3 0.0 copy-done.1
  286.3 0.0 copy-done.4
  286.3 4.6 fusion.28
  290.9 0.0 copy-start.6
  290.9 0.2 concatenate.27
  291.1 1.3 fusion.29
  292.4 1.1 pad_maximum_fusion
  293.5 0.0 all-gather.4.cloned.1.call-done
  293.5 0.0 copy-done.6
  293.5 11.8 %fusion.11 = (f32[4096]{0:T(1024)S(1)}, f32[512]{0:T(512)S(1)}, f32[512,4096]{1,0:T(8,128)}) fusion(bf16[1,512,4096]{2,1,0:T(8,128)(2,1)} %param.8, f32[512]{0:T(512)S(1)} %add_rsqrt_fusion, f32[4096]{0:T(1024)S(1)} %bitcast.70, bf16[1,4096,1024]{2,1,0:T(8,128)(2,1)} %all-gather.4.cloned.1.call-done, bf16[512,512]{1,0:T(8,128)(2,1)S(1)} %copy-done.6, ...), kind=kOutput, calls=%fused_computation.13 | convolution fusion | flops 4311739904 | bytes 22056960 | tf_op jit(solution)/shard_map/dot_general | solution.py:44
  305.3 153.3 %all-reduce = f32[4096]{0:T(1024)S(1)} all-reduce(f32[4096]{0:T(1024)S(1)} %broadcast_multiply_fusion.2), channel_id=5, replica_groups=mesh['replica'=4,'fsdp'=32] {'fsdp'}, use_global_device_ids=true, to_apply=%region_4.5.clone | all-reduce | flops 4096 | bytes 32768
  458.6 0.6 dynamic-slice_bitcast_fusion
  459.2 7.3 %fusion.21 = bf16[1,512,4096]{2,1,0:T(8,128)(2,1)} fusion(bf16[1,512,4096]{2,1,0:T(8,128)(2,1)} %param.8, f32[512,4096]{1,0:T(8,128)} %get-tuple-element.23, f32[512]{0:T(512)S(1)} %broadcast_multiply_fusion.3, f32[4096]{0:T(1024)S(1)} %bitcast.71, f32[512]{0:T(512)S(1)} %add_rsqrt_fusion), kind=kLoop, calls=%fused_computation.22 | loop fusion | flops 14680064 | bytes 16797696 | tf_op jit(solution)/shard_map/broadcast_in_dim | solution.py:115
  466.5 21.4 %reduce-scatter.2.cloned.1.call-done = f32[128,1024]{1,0:T(8,128)} async-done(((f32[4096,1024]{1,0:T(8,128)}), f32[128,1024]{1,0:T(8,128)}) %reduce-scatter.2.cloned.1.call-update) | async-done | bytes 524304 | tf_op jit(solution)/shard_map/reduce_scatter | solution.py:97
  (6 shorter events, 0.1 us)
Async XLA Ops:
  8.0 278.3 %all-reduce.3.cloned.1.call-start = ((), (), s32[]{:S(2)}) async-start(), calls=%async_computation.3 | async-start | bytes 3145728 | tf_op jit(solution)/shard_map/psum | solution.py:106
  8.7 284.8 %all-gather.4.cloned.1.call-start = ((), (), s32[]{:S(2)}) async-start(), calls=%async_computation.4 | async-start | bytes 8650752 | tf_op jit(solution)/shard_map/all_gather | solution.py:83
  14.6 9.6 %copy-start.7 = (bf16[1,128]{1,0:T(2,128)(2,1)S(1)}, bf16[1,128]{1,0:T(2,128)(2,1)}, u32[]{:S(2)}) copy-start(bf16[1,128]{1,0:T(2,128)(2,1)} %param.9) | copy-start | bytes 772
  14.6 240.8 %copy-start.3 = (bf16[1,512,1024]{2,1,0:T(8,128)(2,1)S(1)}, bf16[1,512,1024]{2,1,0:T(8,128)(2,1)}, u32[]{:S(2)}) copy-start(bf16[1,512,1024]{2,1,0:T(8,128)(2,1)} %param.11) | copy-start | bytes 3145732
  14.6 247.2 %all-to-all-start = ((bf16[32,128,1024]{2,1,0:T(8,128)(2,1)}), bf16[32,128,1024]{2,1,0:T(8,128)(2,1)}, u32[]{:S(2)}, u32[]{:S(2)}) async-start(bf16[32,128,1024]{2,1,0:T(8,128)(2,1)} %stack.3), calls=%async_computation | async-start | bytes 16777216 | tf_op jit(solution)/shard_map/all_to_all | solution.py:79
  24.1 463.8 %reduce-scatter.2.cloned.1.call-start = ((), (), s32[]{:S(2)}) async-start(), calls=%async_computation.2 | async-start | bytes 17301504 | tf_op jit(solution)/shard_map/reduce_scatter | solution.py:97
  270.0 1.3 copy-start.2
  271.8 4.3 copy-start
  271.8 4.3 copy-start.5
  284.4 0.7 copy-start.8
  284.4 1.9 copy-start.1
  284.4 1.9 copy-start.4
  290.9 2.6 copy-start.6
Sparse Core Ops, SparseCore 0:
  11.3 175.1 all-reduce.2
Sparse Core Ops, SparseCore 1:
  10.9 244.1 all-gather.3
  284.5 203.3 reduce-scatter.1
